TPU v7x, 32 devices: a whole 2x2x4 slice. The times are simulated.
32 devices in a mesh: grp: 2 (over x), seq: 16 (over z, y, core).
Axes of the slice: x: 2, y: 2, z: 4, core: 2. Of those that a mesh axis runs over, the one named last changes fastest.
Arguments:
- signal: bfloat16 [32768, 768], P(('grp', 'seq')), parts along dimension 0, may hold values from -6 to 6
- dilated_tap_weight: bfloat16 [4, 3, 768, 384], replicated, may hold values from -0.125 to 0.125
- point_weight: bfloat16 [4, 384, 768], replicated, may hold values from -0.3125 to 0.3125
Outputs:
- activations: bfloat16 [4, 32768, 768], P(None, ('grp', 'seq')), parts along dimension 1
There are 2 independent parts, one for each index of `grp`. A program takes and returns all parts, laid end to end along the dimension named above; an argument that names none is the same for every part. Nothing has to cross between parts.
All inputs are finite; a program needn't handle non-finite values.
Results may differ from a plain program's by a relative error of at most 0.0075.
Values may be sent and summed in bfloat16 or wider, within the bound.
A program may use at most 64 MiB of HBM per device.

v0:
```python
import jax
import jax.numpy as jnp
from jax import lax
from jax.sharding import PartitionSpec as P

FIRST_DILATION = 256


def passed_along(value, axis, by):
    size = lax.axis_size(axis)
    pairs = [(i, i + by) for i in range(size) if 0 <= i + by < size]
    return lax.ppermute(value, axis, pairs)


def move_sides(lower_tap_source, high_source, dilation_step):
    length = lower_tap_source.shape[0]
    if dilation_step < length:
        lower = passed_along(lower_tap_source[length - dilation_step :], "seq", 1)
        upper = passed_along(high_source[:dilation_step], "seq", -1)
        lower_neighbour_rows = jnp.concatenate(
            [lower, lower_tap_source[: length - dilation_step]], axis=0
        )
        above_side = jnp.concatenate([high_source[dilation_step:], upper], axis=0)
        return (lower_neighbour_rows, above_side)
    distance = dilation_step // length
    lower_neighbour_rows = passed_along(lower_tap_source, "seq", distance)
    above_side = passed_along(high_source, "seq", -distance)
    return (lower_neighbour_rows, above_side)


def shards(signal, dilated_tap_weight, point_weight):
    current = signal
    outputs = []
    for block_layer_index in range(dilated_tap_weight.shape[0]):
        dilation_step = FIRST_DILATION * 2**block_layer_index
        low_terms = jnp.dot(
            current, dilated_tap_weight[block_layer_index, 0], preferred_element_type=jnp.float32
        ).astype(jnp.bfloat16)
        upper_tap_terms = jnp.dot(
            current, dilated_tap_weight[block_layer_index, 2], preferred_element_type=jnp.float32
        ).astype(jnp.bfloat16)
        below_terms, above_terms = move_sides(low_terms, upper_tap_terms, dilation_step)
        convolved = jnp.dot(
            current, dilated_tap_weight[block_layer_index, 1], preferred_element_type=jnp.float32
        )
        convolved = convolved + below_terms.astype(jnp.float32)
        convolved = convolved + above_terms.astype(jnp.float32)
        hidden = jax.nn.gelu(convolved, approximate=True).astype(jnp.bfloat16)
        residual_branch = jnp.dot(
            hidden, point_weight[block_layer_index], preferred_element_type=jnp.float32
        )
        current = (current.astype(jnp.float32) + residual_branch).astype(jnp.bfloat16)
        outputs.append(current)
    return jnp.stack(outputs)


def solution(mesh):
    in_specs = (P(("grp", "seq"), None), P(), P())
    out_specs = P(None, ("grp", "seq"), None)
    return jax.shard_map(shards, mesh=mesh, in_specs=in_specs, out_specs=out_specs, check_vma=False)
```

profile of v0, /device:TPU:15, one launch (start us, length us, event | category | flops | bytes accessed | tf_op | source)
XLA Modules:
  0.0 127.5 jit_solution(15200863757853966297)
XLA Ops:
  0.0 2.6 %convolution_convert_fusion.6 = bf16[1024,384]{1,0:T(8,128)(2,1)S(1)} fusion(bf16[1024,768]{1,0:T(8,128)(2,1)} %param.3, bf16[4,3,768,384]{3,2,1,0:T(8,128)(2,1)} %param.4), kind=kOutput, calls=%fused_computation.48 | convolution fusion | flops 604372992 | bytes 2949120 | tf_op jit(solution)/shard_map/dot_general | solution.py:39
  2.7 2.6 %collective-permute-start.1 = (bf16[256,384]{1,0:T(8,128)(2,1)S(1)}, bf16[256,384]{1,0:T(8,128)(2,1)S(1)}, u32[]{:S(2)}, u32[]{:S(2)}) collective-permute-start(bf16[256,384]{1,0:T(8,128)(2,1)S(1)} %slice.99), channel_id=1, source_target_pairs={{1,0},{2,1},{3,2},{4,3},{5,4},{6,5},{7,6},{8,7},{9,8},{10,9},{11,1... | collective-permute-start | bytes 589832 | tf_op jit(solution)/shard_map/ppermute | solution.py:12
  5.3 2.0 %convolution_convert_fusion.7 = bf16[1024,384]{1,0:T(8,128)(2,1)S(1)} fusion(bf16[1024,768]{1,0:T(8,128)(2,1)S(1)} %copy-done.1, bf16[4,3,768,384]{3,2,1,0:T(8,128)(2,1)} %param.4), kind=kOutput, calls=%fused_computation.49 | convolution fusion | flops 604372992 | bytes 2949120 | tf_op jit(solution)/shard_map/dot_general | solution.py:36
  7.3 3.9 %collective-permute-start = (bf16[256,384]{1,0:T(8,128)(2,1)S(1)}, bf16[256,384]{1,0:T(8,128)(2,1)S(1)}, u32[]{:S(2)}, u32[]{:S(2)}) collective-permute-start(bf16[256,384]{1,0:T(8,128)(2,1)S(1)} %slice.96), channel_id=1, source_target_pairs={{0,1},{1,2},{2,3},{3,4},{4,5},{5,6},{6,7},{7,8},{8,9},{9,10},{10,1... | collective-permute-start | bytes 589832 | tf_op jit(solution)/shard_map/ppermute | solution.py:12
  11.4 2.4 %collective-permute-done = bf16[256,384]{1,0:T(8,128)(2,1)S(1)} collective-permute-done((bf16[256,384]{1,0:T(8,128)(2,1)S(1)}, bf16[256,384]{1,0:T(8,128)(2,1)S(1)}, u32[]{:S(2)}, u32[]{:S(2)}) %collective-permute-start) | collective-permute-done | bytes 196640 | tf_op jit(solution)/shard_map/ppermute | solution.py:12
  13.8 4.3 %add_convert_fusion.3 = bf16[1024,768]{1,0:T(8,128)(2,1)S(1)} fusion(bf16[1024,768]{1,0:T(8,128)(2,1)} %param.3, bf16[768,384]{1,0:T(8,128)(2,1)S(1)} %slice.97, bf16[256,384]{1,0:T(8,128)(2,1)S(1)} %collective-permute-done, bf16[256,384]{1,0:T(8,128)(2,1)S(1)} %collective-permute-done.1, bf16[768,384]{1,0:T(8,128)(2,1)S(1)} %slice.98, ...), kind=kOutput, calls=%fused_computation.4 | convolution fusion | flops 1217789952 | bytes 7471104 | tf_op jit(solution)/shard_map/dot_general | solution.py:49
  18.1 2.0 %convolution_convert_fusion.5 = bf16[1024,384]{1,0:T(8,128)(2,1)S(1)} fusion(bf16[1024,768]{1,0:T(8,128)(2,1)S(1)} %add_convert_fusion.3, bf16[4,3,768,384]{3,2,1,0:T(8,128)(2,1)} %param.4), kind=kOutput, calls=%fused_computation.47 | convolution fusion | flops 604372992 | bytes 2949120 | tf_op jit(solution)/shard_map/dot_general | solution.py:36
  20.1 2.0 %convolution_convert_fusion.4 = bf16[1024,384]{1,0:T(8,128)(2,1)S(1)} fusion(bf16[1024,768]{1,0:T(8,128)(2,1)S(1)} %add_convert_fusion.3, bf16[4,3,768,384]{3,2,1,0:T(8,128)(2,1)} %param.4), kind=kOutput, calls=%fused_computation.46 | convolution fusion | flops 604372992 | bytes 2949120 | tf_op jit(solution)/shard_map/dot_general | solution.py:39
  22.3 5.3 %collective-permute-start.2 = (bf16[512,384]{1,0:T(8,128)(2,1)S(1)}, bf16[512,384]{1,0:T(8,128)(2,1)S(1)}, u32[]{:S(2)}, u32[]{:S(2)}) collective-permute-start(bf16[512,384]{1,0:T(8,128)(2,1)S(1)} %get-tuple-element.7), channel_id=1, source_target_pairs={{0,1},{1,2},{2,3},{3,4},{4,5},{5,6},{6,7},{7,8},{8,9},{9,10},{10,1... | collective-permute-start | bytes 1179656 | tf_op jit(solution)/shard_map/ppermute | solution.py:12
  32.3 6.1 %collective-permute-done.3 = bf16[512,384]{1,0:T(8,128)(2,1)S(1)} collective-permute-done((bf16[512,384]{1,0:T(8,128)(2,1)S(1)}, bf16[512,384]{1,0:T(8,128)(2,1)S(1)}, u32[]{:S(2)}, u32[]{:S(2)}) %collective-permute-start.3) | collective-permute-done | bytes 393248 | tf_op jit(solution)/shard_map/ppermute | solution.py:12
  39.1 3.6 %add_convert_fusion.2 = bf16[1024,768]{1,0:T(8,128)(2,1)S(1)} fusion(bf16[1024,768]{1,0:T(8,128)(2,1)S(1)} %add_convert_fusion.3, bf16[512,384]{1,0:T(8,128)(2,1)S(1)} %get-tuple-element.8, bf16[512,384]{1,0:T(8,128)(2,1)} %copy-done.2, bf16[512,384]{1,0:T(8,128)(2,1)} %copy-done.3, bf16[512,384]{1,0:T(8,128)(2,1)} %get-tuple-element.5, ...), kind=kOutput, calls=%fused_computation.3 | convolution fusion | flops 1217789952 | bytes 7471104 | tf_op jit(solution)/shard_map/dot_general | solution.py:49
  42.7 2.0 %convolution_convert_fusion.3 = bf16[1024,384]{1,0:T(8,128)(2,1)S(1)} fusion(bf16[1024,768]{1,0:T(8,128)(2,1)S(1)} %add_convert_fusion.2, bf16[4,3,768,384]{3,2,1,0:T(8,128)(2,1)} %param.4), kind=kOutput, calls=%fused_computation.45 | convolution fusion | flops 604372992 | bytes 2949120 | tf_op jit(solution)/shard_map/dot_general | solution.py:36
  44.8 2.0 %convolution_convert_fusion.2 = bf16[1024,384]{1,0:T(8,128)(2,1)S(1)} fusion(bf16[1024,768]{1,0:T(8,128)(2,1)S(1)} %add_convert_fusion.2, bf16[4,3,768,384]{3,2,1,0:T(8,128)(2,1)} %param.4), kind=kOutput, calls=%fused_computation.44 | convolution fusion | flops 604372992 | bytes 2949120 | tf_op jit(solution)/shard_map/dot_general | solution.py:39
  48.8 4.5 %collective-permute-start.4 = (bf16[1024,384]{1,0:T(8,128)(2,1)S(1)}, bf16[1024,384]{1,0:T(8,128)(2,1)}, u32[]{:S(2)}, u32[]{:S(2)}) collective-permute-start(bf16[1024,384]{1,0:T(8,128)(2,1)S(1)} %convolution_convert_fusion.3), channel_id=1, source_target_pairs={{0,1},{1,2},{2,3},{3,4},{4,5},{5,6},{6,7},{7,8},{8,9},{9,10},{10,1... | collective-permute-start | bytes 2359304 | tf_op jit(solution)/shard_map/ppermute | solution.py:12
  53.3 7.9 %collective-permute-done.5 = bf16[1024,384]{1,0:T(8,128)(2,1)} collective-permute-done((bf16[1024,384]{1,0:T(8,128)(2,1)S(1)}, bf16[1024,384]{1,0:T(8,128)(2,1)}, u32[]{:S(2)}, u32[]{:S(2)}) %collective-permute-start.5) | collective-permute-done | bytes 786464 | tf_op jit(solution)/shard_map/ppermute | solution.py:12
  62.3 4.9 %add_convert_fusion.1 = bf16[1024,768]{1,0:T(8,128)(2,1)} fusion(bf16[1024,768]{1,0:T(8,128)(2,1)S(1)} %add_convert_fusion.2, bf16[1024,384]{1,0:T(8,128)(2,1)} %collective-permute-done.5, bf16[1024,384]{1,0:T(8,128)(2,1)} %collective-permute-done.4, bf16[4,384,768]{2,1,0:T(8,128)(2,1)} %param.5, bf16[4,3,768,384]{3,2,1,0:T(8,128)(2,1)} %param.4), kind=kOutput, calls=%fused_computation.2 | convolution fusion | flops 1215430656 | bytes 7471104 | tf_op jit(solution)/shard_map/dot_general | solution.py:49
  67.2 2.6 %convolution_convert_fusion.1 = bf16[1024,384]{1,0:T(8,128)(2,1)S(1)} fusion(bf16[1024,768]{1,0:T(8,128)(2,1)} %add_convert_fusion.1, bf16[4,3,768,384]{3,2,1,0:T(8,128)(2,1)} %param.4), kind=kOutput, calls=%fused_computation.43 | convolution fusion | flops 604372992 | bytes 2949120 | tf_op jit(solution)/shard_map/dot_general | solution.py:36
  69.8 2.0 %convolution_convert_fusion = bf16[1024,384]{1,0:T(8,128)(2,1)S(1)} fusion(bf16[1024,768]{1,0:T(8,128)(2,1)S(1)} %copy-done, bf16[4,3,768,384]{3,2,1,0:T(8,128)(2,1)} %param.4), kind=kOutput, calls=%fused_computation.42 | convolution fusion | flops 604372992 | bytes 2949120 | tf_op jit(solution)/shard_map/dot_general | solution.py:39
  71.9 8.7 %collective-permute-start.7 = (bf16[1024,384]{1,0:T(8,128)(2,1)S(1)}, bf16[1024,384]{1,0:T(8,128)(2,1)}, u32[]{:S(2)}, u32[]{:S(2)}) collective-permute-start(bf16[1024,384]{1,0:T(8,128)(2,1)S(1)} %convolution_convert_fusion), channel_id=1, source_target_pairs={{2,0},{3,1},{4,2},{5,3},{6,4},{7,5},{8,6},{9,7},{10,8},{11,9},{12,... | collective-permute-start | bytes 2359304 | tf_op jit(solution)/shard_map/ppermute | solution.py:12
  80.5 2.9 %collective-permute-start.6 = (bf16[1024,384]{1,0:T(8,128)(2,1)S(1)}, bf16[1024,384]{1,0:T(8,128)(2,1)}, u32[]{:S(2)}, u32[]{:S(2)}) collective-permute-start(bf16[1024,384]{1,0:T(8,128)(2,1)S(1)} %convolution_convert_fusion.1), channel_id=1, source_target_pairs={{0,2},{1,3},{2,4},{3,5},{4,6},{5,7},{6,8},{7,9},{8,10},{9,11},{10,... | collective-permute-start | bytes 2359304 | tf_op jit(solution)/shard_map/ppermute | solution.py:12
  83.5 29.8 %collective-permute-done.7 = bf16[1024,384]{1,0:T(8,128)(2,1)} collective-permute-done((bf16[1024,384]{1,0:T(8,128)(2,1)S(1)}, bf16[1024,384]{1,0:T(8,128)(2,1)}, u32[]{:S(2)}, u32[]{:S(2)}) %collective-permute-start.7) | collective-permute-done | bytes 786464 | tf_op jit(solution)/shard_map/ppermute | solution.py:12
  113.3 3.2 %collective-permute-done.6 = bf16[1024,384]{1,0:T(8,128)(2,1)} collective-permute-done((bf16[1024,384]{1,0:T(8,128)(2,1)S(1)}, bf16[1024,384]{1,0:T(8,128)(2,1)}, u32[]{:S(2)}, u32[]{:S(2)}) %collective-permute-start.6) | collective-permute-done | bytes 786464 | tf_op jit(solution)/shard_map/ppermute | solution.py:12
  116.5 5.9 %fusion.32 = bf16[1,1024,768]{2,1,0:T(8,128)(2,1)} fusion(bf16[1024,768]{1,0:T(8,128)(2,1)} %add_convert_fusion.1, bf16[1024,384]{1,0:T(8,128)(2,1)} %collective-permute-done.7, bf16[1024,384]{1,0:T(8,128)(2,1)} %collective-permute-done.6, bf16[4,384,768]{2,1,0:T(8,128)(2,1)} %param.5, bf16[4,3,768,384]{3,2,1,0:T(8,128)(2,1)} %param.4), kind=kOutput, calls=%fused_computation.41 | convolution fusion | flops 1215430656 | bytes 7471104 | tf_op jit(solution)/shard_map/dot_general | solution.py:49
  122.4 5.1 %pad_maximum_fusion = bf16[4,1024,768]{2,1,0:T(8,128)(2,1)} fusion(bf16[1,1024,768]{2,1,0:T(8,128)(2,1)} %fusion.32, bf16[1,1024,768]{2,1,0:T(8,128)(2,1)} %bitcast.83, bf16[1,1024,768]{2,1,0:T(8,128)(2,1)S(1)} %bitcast.82, bf16[1,1024,768]{2,1,0:T(8,128)(2,1)S(1)} %bitcast.81), kind=kLoop, calls=%fused_computation | loop fusion | flops 9437184 | bytes 12582912 | tf_op jit(solution)/shard_map/stack | solution.py:54
  (19 shorter events, 8.7 us)
Async XLA Ops:
  0.0 5.3 %copy-start.1 = (bf16[1024,768]{1,0:T(8,128)(2,1)S(1)}, bf16[1024,768]{1,0:T(8,128)(2,1)}, u32[]{:S(2)}) copy-start(bf16[1024,768]{1,0:T(8,128)(2,1)} %param.3) | copy-start | bytes 4718596
  2.7 8.7 %collective-permute-start.1 = (bf16[256,384]{1,0:T(8,128)(2,1)S(1)}, bf16[256,384]{1,0:T(8,128)(2,1)S(1)}, u32[]{:S(2)}, u32[]{:S(2)}) collective-permute-start(bf16[256,384]{1,0:T(8,128)(2,1)S(1)} %slice.99), channel_id=1, source_target_pairs={{1,0},{2,1},{3,2},{4,3},{5,4},{6,5},{7,6},{8,7},{9,8},{10,9},{11,1... | collective-permute-start | bytes 589832 | tf_op jit(solution)/shard_map/ppermute | solution.py:12
  7.3 6.5 %collective-permute-start = (bf16[256,384]{1,0:T(8,128)(2,1)S(1)}, bf16[256,384]{1,0:T(8,128)(2,1)S(1)}, u32[]{:S(2)}, u32[]{:S(2)}) collective-permute-start(bf16[256,384]{1,0:T(8,128)(2,1)S(1)} %slice.96), channel_id=1, source_target_pairs={{0,1},{1,2},{2,3},{3,4},{4,5},{5,6},{6,7},{7,8},{8,9},{9,10},{10,1... | collective-permute-start | bytes 589832 | tf_op jit(solution)/shard_map/ppermute | solution.py:12
  22.3 10.0 %collective-permute-start.2 = (bf16[512,384]{1,0:T(8,128)(2,1)S(1)}, bf16[512,384]{1,0:T(8,128)(2,1)S(1)}, u32[]{:S(2)}, u32[]{:S(2)}) collective-permute-start(bf16[512,384]{1,0:T(8,128)(2,1)S(1)} %get-tuple-element.7), channel_id=1, source_target_pairs={{0,1},{1,2},{2,3},{3,4},{4,5},{5,6},{6,7},{7,8},{8,9},{9,10},{10,1... | collective-permute-start | bytes 1179656 | tf_op jit(solution)/shard_map/ppermute | solution.py:12
  28.4 10.0 %collective-permute-start.3 = (bf16[512,384]{1,0:T(8,128)(2,1)S(1)}, bf16[512,384]{1,0:T(8,128)(2,1)S(1)}, u32[]{:S(2)}, u32[]{:S(2)}) collective-permute-start(bf16[512,384]{1,0:T(8,128)(2,1)S(1)} %get-tuple-element.6), channel_id=1, source_target_pairs={{1,0},{2,1},{3,2},{4,3},{5,4},{6,5},{7,6},{8,7},{9,8},{10,9},{11,1... | collective-permute-start | bytes 1179656 | tf_op jit(solution)/shard_map/ppermute | solution.py:12
  32.3 6.1 %copy-start.2 = (bf16[512,384]{1,0:T(8,128)(2,1)}, bf16[512,384]{1,0:T(8,128)(2,1)S(1)}, u32[]{:S(2)}) copy-start(bf16[512,384]{1,0:T(8,128)(2,1)S(1)} %collective-permute-done.2) | copy-start | bytes 1179652
  38.4 0.7 copy-start.3
  46.8 14.4 %collective-permute-start.5 = (bf16[1024,384]{1,0:T(8,128)(2,1)S(1)}, bf16[1024,384]{1,0:T(8,128)(2,1)}, u32[]{:S(2)}, u32[]{:S(2)}) collective-permute-start(bf16[1024,384]{1,0:T(8,128)(2,1)S(1)} %convolution_convert_fusion.2), channel_id=1, source_target_pairs={{1,0},{2,1},{3,2},{4,3},{5,4},{6,5},{7,6},{8,7},{9,8},{10,9},{11,1... | collective-permute-start | bytes 2359304 | tf_op jit(solution)/shard_map/ppermute | solution.py:12
  48.8 13.5 %collective-permute-start.4 = (bf16[1024,384]{1,0:T(8,128)(2,1)S(1)}, bf16[1024,384]{1,0:T(8,128)(2,1)}, u32[]{:S(2)}, u32[]{:S(2)}) collective-permute-start(bf16[1024,384]{1,0:T(8,128)(2,1)S(1)} %convolution_convert_fusion.3), channel_id=1, source_target_pairs={{0,1},{1,2},{2,3},{3,4},{4,5},{5,6},{6,7},{7,8},{8,9},{9,10},{10,1... | collective-permute-start | bytes 2359304 | tf_op jit(solution)/shard_map/ppermute | solution.py:12
  67.2 2.6 %copy-start = (bf16[1024,768]{1,0:T(8,128)(2,1)S(1)}, bf16[1024,768]{1,0:T(8,128)(2,1)}, u32[]{:S(2)}) copy-start(bf16[1024,768]{1,0:T(8,128)(2,1)} %add_convert_fusion.1) | copy-start | bytes 4718596
  71.9 41.4 %collective-permute-start.7 = (bf16[1024,384]{1,0:T(8,128)(2,1)S(1)}, bf16[1024,384]{1,0:T(8,128)(2,1)}, u32[]{:S(2)}, u32[]{:S(2)}) collective-permute-start(bf16[1024,384]{1,0:T(8,128)(2,1)S(1)} %convolution_convert_fusion), channel_id=1, source_target_pairs={{2,0},{3,1},{4,2},{5,3},{6,4},{7,5},{8,6},{9,7},{10,8},{11,9},{12,... | collective-permute-start | bytes 2359304 | tf_op jit(solution)/shard_map/ppermute | solution.py:12
  80.5 36.0 %collective-permute-start.6 = (bf16[1024,384]{1,0:T(8,128)(2,1)S(1)}, bf16[1024,384]{1,0:T(8,128)(2,1)}, u32[]{:S(2)}, u32[]{:S(2)}) collective-permute-start(bf16[1024,384]{1,0:T(8,128)(2,1)S(1)} %convolution_convert_fusion.1), channel_id=1, source_target_pairs={{0,2},{1,3},{2,4},{3,5},{4,6},{5,7},{6,8},{7,9},{8,10},{9,11},{10,... | collective-permute-start | bytes 2359304 | tf_op jit(solution)/shard_map/ppermute | solution.py:12
where the time goes:
time: 128 us; the launch traced here: 127 us
  waiting for transfers between devices  52.5 us (41%)
  matrix products  36.2 us (28%)
  starting transfers between devices  31.7 us (25%)
  other arithmetic  5.08 us (4%)
  local copies, waits for them, and re-layouts  1.82 us (1%)
    ppermute x8, waiting for transfers between devices, passed_along(): return lax.ppermute(value, axis, pairs)  52.5 us
    ppermute x8, starting transfers between devices, passed_along(): return lax.ppermute(value, axis, pairs)  31.7 us
    dot_general x4, matrix products, shards(): jnp.dot(hidden, point_weight[block_layer_index], preferred_element_type=j...  18.7 us
    dot_general x4, matrix products, shards(): jnp.dot(current, dilated_tap_weight[block_layer_index, 0], preferred_elem...  8.73 us
    dot_general x4, matrix products, shards(): jnp.dot(current, dilated_tap_weight[block_layer_index, 2], preferred_elem...  8.73 us
    another operation x1, other arithmetic, shards(): return jnp.stack(outputs)  5.08 us
  transfers between devices with their start and end apart: 8, of which 7 were waited for; matrix products, arithmetic and copies ran while one was open for 2% of the time, Pallas kernels for 0%

commit v1 on v0

v1 whole, which is shorter than its diff:
```python
import functools

import jax
import jax.numpy as jnp
from jax import lax
from jax.experimental import pallas as pl
from jax.experimental.pallas import tpu as pltpu
from jax.sharding import PartitionSpec as P

FIRST_DILATION = 256
MESH = pl.DeviceIdType.MESH


def edges_first(count):
    order = []
    for i in range((count + 1) // 2):
        order.append(i)
        if count - 1 - i != i:
            order.append(count - 1 - i)
    return order


def kernel(n, steps, x_hbm, w_hbm, p_hbm, out_hbm, xs, wv, pv, cen, own, lt, rt, rl, rr,
           send_l, send_r, recv_l, recv_r, sem_x, sem_w, sem_p, sem_o):
    blocks = len(steps)
    chunks, rows = xs.shape[1], xs.shape[2]
    hid = p_hbm.shape[1]
    me = lax.axis_index("seq")

    def relay(b):
        return steps[b] > chunks

    def places(b):
        hop = steps[b] // chunks
        odd = lax.rem(lax.div(me, hop), 2)
        partner = me + hop - 2 * hop * odd
        target = me - 2 * hop + 4 * hop * odd
        source = me + 2 * hop - 4 * hop * odd
        return odd, partner, target, source

    def inside(place):
        return jnp.logical_and(place >= 0, place < n)

    greeted = [me - 1, me + 1]
    for b in range(blocks):
        if relay(b):
            _, partner, target, source = places(b)
            greeted += [partner, target, source]
    barrier = pltpu.get_barrier_semaphore()
    for place in greeted:
        @pl.when(inside(place))
        def _():
            pl.semaphore_signal(barrier, inc=1, device_id={"seq": place}, device_id_type=MESH)

    first = edges_first(chunks)
    def x_load(c):
        return pltpu.make_async_copy(x_hbm.at[pl.ds(c * rows, rows)], xs.at[0, c], sem_x.at[c])

    def w_load(b, t):
        source = t
        if relay(b) and t != 1:
            odd = places(b)[0]
            source = 2 - 2 * odd if t == 0 else 2 * odd
        return pltpu.make_async_copy(
            w_hbm.at[b, source], wv.at[b, :, pl.ds(t * hid, hid)], sem_w.at[b, t])

    def p_load(b):
        return pltpu.make_async_copy(p_hbm.at[b], pv.at[b], sem_p.at[b])

    x_load(first[0]).start()
    for t in range(3):
        w_load(0, t).start()
    for c in first[1:]:
        x_load(c).start()
    p_load(0).start()
    for b in range(1, blocks):
        for t in range(3):
            w_load(b, t).start()
        p_load(b).start()

    @pl.when(me == 0)
    def _():
        for b in range(blocks):
            if not relay(b):
                rl[b] = jnp.zeros(rl.shape[1:], rl.dtype)

    @pl.when(me == n - 1)
    def _():
        for b in range(blocks):
            if not relay(b):
                rr[b] = jnp.zeros(rr.shape[1:], rr.dtype)

    for b in range(blocks):
        if relay(b):
            @pl.when(jnp.logical_not(inside(places(b)[3])))
            def _():
                rl[b] = jnp.zeros(rl.shape[1:], rl.dtype)

    def left_copy(b, s, d, place):
        return pltpu.make_async_remote_copy(
            src_ref=lt.at[b, s], dst_ref=rl.at[b, d], send_sem=send_l.at[b, s],
            recv_sem=recv_l.at[b, d], device_id={"seq": place}, device_id_type=MESH)

    def right_copy(b, s, d, place):
        return pltpu.make_async_remote_copy(
            src_ref=rt.at[b, s], dst_ref=rr.at[b, d], send_sem=send_r.at[b, s],
            recv_sem=recv_r.at[b, d], device_id={"seq": place}, device_id_type=MESH)

    sent = []

    def send(copy, place, guarded):
        if not guarded:
            copy.start()
            sent.append((copy, None))
            return

        @pl.when(inside(place))
        def _():
            copy.start()
        sent.append((copy, place))

    def taps(b, c):
        if b == 0:
            x_load(c).wait()
        if taps_done[b] == 0:
            for t in range(3):
                w_load(b, t).wait()
        taps_done[b] += 1
        y = jnp.dot(xs[b, c], wv[b], preferred_element_type=jnp.float32)
        lt[b, c] = y[:, :hid].astype(lt.dtype)
        cen[c] = y[:, hid:2 * hid]
        if relay(b):
            own[c] = y[:, 2 * hid:]
        else:
            rt[b, c] = y[:, 2 * hid:].astype(rt.dtype)
        if b == 0 and taps_done[b] == 1:
            peers = sum(inside(place).astype(jnp.int32) for place in greeted)
            pl.semaphore_wait(barrier, peers)
        if relay(b):
            target = places(b)[2]
            send(left_copy(b, c, c, target), target, True)
            return
        step = steps[b]
        if c + step >= chunks:
            send(left_copy(b, c, c + step - chunks, me + 1), me + 1, True)
        if c < step:
            send(right_copy(b, c, c - step + chunks, me - 1), me - 1, True)

    def pass_on(b, c):
        _, partner, target, source = places(b)

        @pl.when(inside(source))
        def _():
            left_copy(b, c, c, target).wait_recv()
        rt[b, c] = (own[c] + rl[b, c].astype(jnp.float32)).astype(rt.dtype)
        send(right_copy(b, c, c, partner), partner, False)

    def mix(b, c):
        v = cen[c]
        if relay(b):
            right_copy(b, c, c, places(b)[1]).wait_recv()
            v = v + rr[b, c].astype(jnp.float32)
        else:
            step = steps[b]
            if c >= step:
                v = v + lt[b, c - step].astype(jnp.float32)
            else:
                @pl.when(me > 0)
                def _():
                    left_copy(b, c - step + chunks, c, me + 1).wait_recv()
                v = v + rl[b, c].astype(jnp.float32)
            if c + step < chunks:
                v = v + rt[b, c + step].astype(jnp.float32)
            else:
                @pl.when(me < n - 1)
                def _():
                    right_copy(b, c + step - chunks, c, me - 1).wait_recv()
                v = v + rr[b, c].astype(jnp.float32)
        if mix_done[b] == 0:
            p_load(b).wait()
        mix_done[b] += 1
        hidden = jax.nn.gelu(v, approximate=True).astype(jnp.bfloat16)
        branch = jnp.dot(hidden, pv[b], preferred_element_type=jnp.float32)
        xs[b + 1, c] = (xs[b, c].astype(jnp.float32) + branch).astype(xs.dtype)
        out_copy(b, c).start()

    def out_copy(b, c):
        return pltpu.make_async_copy(
            xs.at[b + 1, c], out_hbm.at[b, pl.ds(c * rows, rows)], sem_o.at[b, c])

    taps_done = [0] * blocks
    mix_done = [0] * blocks
    unpassed = []
    for c in first:
        taps(0, c)
    for b in range(blocks):
        order = first
        if steps[b] < chunks:
            order = sorted(first, key=lambda c: (c < steps[b]) + (c + steps[b] >= chunks))
        for i, c in enumerate(order):
            mix(b, c)
            if relay(b) and unpassed:
                pass_on(b, unpassed.pop(0))
            if b + 1 < blocks:
                taps(b + 1, c)
                if relay(b + 1):
                    if i:
                        pass_on(b + 1, unpassed.pop(0))
                    unpassed.append(c)

    for copy, place in sent:
        if place is None:
            copy.wait_send()
        else:
            @pl.when(inside(place))
            def _():
                copy.wait_send()
    for b in range(blocks):
        for c in range(chunks):
            out_copy(b, c).wait()


def shards(n, signal, dilated_tap_weight, point_weight):
    length, wide = signal.shape
    blocks, taps, _, hid = dilated_tap_weight.shape
    rows = min(FIRST_DILATION, length)
    chunks = length // rows
    steps = [FIRST_DILATION * 2**b // rows for b in range(blocks)]
    for step in steps:
        hop = step // chunks
        assert step <= chunks or (step % chunks == 0 and n % (2 * hop) == 0)
    bf16, f32 = jnp.bfloat16, jnp.float32
    terms = pltpu.VMEM((blocks, chunks, rows, hid), bf16)
    dma = pltpu.SemaphoreType.DMA
    return pl.pallas_call(
        functools.partial(kernel, n, steps),
        out_shape=jax.ShapeDtypeStruct((blocks, length, wide), bf16),
        in_specs=[pl.BlockSpec(memory_space=pl.ANY)] * 3,
        out_specs=pl.BlockSpec(memory_space=pl.ANY),
        scratch_shapes=[
            pltpu.VMEM((blocks + 1, chunks, rows, wide), bf16),
            pltpu.VMEM((blocks, wide, taps * hid), bf16),
            pltpu.VMEM((blocks, hid, wide), bf16),
            pltpu.VMEM((chunks, rows, hid), f32),
            pltpu.VMEM((chunks, rows, hid), f32),
            terms, terms, terms, terms,
            dma((blocks, chunks)), dma((blocks, chunks)),
            dma((blocks, chunks)), dma((blocks, chunks)),
            dma((chunks,)), dma((blocks, taps)), dma((blocks,)), dma((blocks, chunks)),
        ],
        compiler_params=pltpu.CompilerParams(
            collective_id=0, has_side_effects=True, vmem_limit_bytes=56 * 2**20),
    )(signal, dilated_tap_weight, point_weight)


def solution(mesh):
    in_specs = (P(("grp", "seq"), None), P(), P())
    out_specs = P(None, ("grp", "seq"), None)
    return jax.shard_map(functools.partial(shards, mesh.shape["seq"]), mesh=mesh,
                         in_specs=in_specs, out_specs=out_specs, check_vma=False)
```

time: 128 us -> 61.4 us (0.48)
  Pallas kernels: 0 us -> 55.3 us
  waiting for transfers between devices: 52.5 us -> 0 us
  matrix products: 36.2 us -> 0 us
  starting transfers between devices: 31.7 us -> 0 us
  other arithmetic: 5.08 us -> 0 us
  local copies, waits for them, and re-layouts: 1.82 us -> 5.89 us
    pallas_call x0 -> x1, Pallas kernels: none -> 55.3 us  [shards(): pl.pallas_call(functools.partial(kernel, n, steps), out_shape=jax.ShapeDt...]
    ppermute x8 -> x0, waiting for transfers between devices: 52.5 us -> none  [passed_along(): return lax.ppermute(value, axis, pairs)]
    dot_general x12 -> x0, matrix products: 36.2 us -> none  [the longest x4 18.7 us: shards(): jnp.dot(hidden, point_weight[block_layer_index], preferred_element_type=j...]
    ppermute x8 -> x0, starting transfers between devices: 31.7 us -> none  [passed_along(): return lax.ppermute(value, axis, pairs)]
    unnamed x8 -> x1, local copies, waits for them, and re-layouts: 0.76 us -> 5.89 us
    another operation x1 -> x0, other arithmetic: 5.08 us -> none  [shards(): return jnp.stack(outputs)]
  transfers between devices with their start and end apart: 8 -> 0, of which waited for: 7 -> 0; matrix products, arithmetic and copies ran while one was open for 2% -> 0% of each run, Pallas kernels for 0% -> 0%
where the time goes in v1:
time: 61.4 us; the launch traced here: 61.2 us
  Pallas kernels  55.3 us (90%)
  local copies, waits for them, and re-layouts  5.89 us (10%)
    pallas_call x1, Pallas kernels, shards(): pl.pallas_call(functools.partial(kernel, n, steps), out_shape=jax.ShapeDt...  55.3 us
    unnamed x1, local copies, waits for them, and re-layouts  5.89 us

profile of v1, /device:TPU:15, one launch (start us, length us, event | category | flops | bytes accessed | tf_op | source)
XLA Modules:
  0.0 61.2 jit_solution(4131405559887243666)
XLA Ops:
  0.0 55.3 %shard_map.37 = bf16[4,1024,768]{2,1,0:T(8,128)(2,1)} custom-call(bf16[1024,768]{1,0:T(8,128)(2,1)} %x_hbm.1, bf16[4,3,768,384]{3,2,1,0:T(8,128)(2,1)} %w_hbm.1, bf16[4,384,768]{2,1,0:T(8,128)(2,1)} %p_hbm.1), custom_call_target="tpu_custom_call" | custom-call | tf_op jit(solution)/shard_map/pallas_call | solution.py:235
  55.3 5.9 %copy.5 = bf16[4,1024,768]{2,1,0:T(8,128)(2,1)} copy(bf16[4,1024,768]{2,1,0:T(8,128)(2,1)} %shard_map.37) | data formatting | bytes 12582912

commit v2 on v1

v2 whole, which is shorter than its diff:
```python
import functools

import jax
import jax.numpy as jnp
from jax import lax
from jax.experimental import pallas as pl
from jax.experimental.pallas import tpu as pltpu
from jax.sharding import PartitionSpec as P

FIRST_DILATION = 256
MESH = pl.DeviceIdType.MESH


def edges_first(count):
    order = []
    for i in range((count + 1) // 2):
        order.append(i)
        if count - 1 - i != i:
            order.append(count - 1 - i)
    return order


def kernel(n, steps, x_hbm, w_hbm, p_hbm, out, xs, wv, pv, cen, own, to, ti, ro, ri,
           send_o, send_i, recv_o, recv_i, sem_x, sem_w, sem_p):
    blocks = len(steps)
    chunks, rows = xs.shape[0], xs.shape[1]
    hid = p_hbm.shape[1]
    me = lax.axis_index("seq")
    core = lax.rem(me, 2)
    outer = me - 1 + 2 * core
    inner = me + 1 - 2 * core

    def relay(b):
        return steps[b] > chunks

    def places(b):
        hop = steps[b] // chunks
        odd = lax.rem(lax.div(me, hop), 2)
        partner = me + hop - 2 * hop * odd
        target = me - 2 * hop + 4 * hop * odd
        source = me + 2 * hop - 4 * hop * odd
        return odd, partner, target, source

    def inside(place):
        return jnp.logical_and(place >= 0, place < n)

    greeted = [outer, inner]
    for b in range(blocks):
        if relay(b):
            _, partner, target, source = places(b)
            greeted += [partner, target, source]
    barrier = pltpu.get_barrier_semaphore()
    for place in greeted:
        @pl.when(inside(place))
        def _():
            pl.semaphore_signal(barrier, inc=1, device_id={"seq": place}, device_id_type=MESH)

    def span(c):
        at = (c + core * (chunks - 1 - 2 * c)) * rows
        return pl.ds(pl.multiple_of(at, rows), rows)

    def x_load(c):
        return pltpu.make_async_copy(x_hbm.at[span(c)], xs.at[c], sem_x.at[c])

    def w_load(b, t):
        side = places(b)[0] if relay(b) else core
        source = (2 - 2 * side, 1, 2 * side)[t]
        return pltpu.make_async_copy(
            w_hbm.at[b, source], wv.at[b, :, pl.ds(t * hid, hid)], sem_w.at[b, t])

    def p_load(b):
        return pltpu.make_async_copy(p_hbm.at[b], pv.at[b], sem_p.at[b])

    x_load(0).start()
    for t in range(3):
        w_load(0, t).start()
    for c in range(1, chunks):
        x_load(c).start()
    p_load(0).start()
    for b in range(1, blocks):
        for t in range(3):
            w_load(b, t).start()
        p_load(b).start()

    def fill_ends():
        for b in range(blocks):
            source = places(b)[3] if relay(b) else outer

            @pl.when(jnp.logical_not(inside(source)))
            def _():
                for c in range(min(steps[b], chunks)):
                    ro[b, c] = jnp.zeros(ro.shape[2:], ro.dtype)

    def outer_copy(b, s, d, place):
        return pltpu.make_async_remote_copy(
            src_ref=to.at[b, s], dst_ref=ro.at[b, d], send_sem=send_o.at[b, s],
            recv_sem=recv_o.at[b, d], device_id={"seq": place}, device_id_type=MESH)

    def inner_copy(b, s, d, place):
        return pltpu.make_async_remote_copy(
            src_ref=ti.at[b, s], dst_ref=ri.at[b, d], send_sem=send_i.at[b, s],
            recv_sem=recv_i.at[b, d], device_id={"seq": place}, device_id_type=MESH)

    sent = []

    def send(copy, place=None):
        if place is None:
            copy.start()
        else:
            @pl.when(inside(place))
            def _():
                copy.start()
        sent.append((copy, place))

    def x_of(b, c):
        return xs[c] if b == 0 else out[b - 1, span(c), :]

    def send_outer(b, c):
        if relay(b):
            target = places(b)[2]
            send(outer_copy(b, c, c, target), target)
        elif c < steps[b]:
            send(outer_copy(b, c, steps[b] - 1 - c, outer), outer)

    loaded = set()

    def once(load, *key):
        if (load, key) not in loaded:
            loaded.add((load, key))
            load(*key).wait()

    def taps(b, c):
        if b == 0:
            x_load(c).wait()
        x = x_of(b, c)
        once(w_load, b, 0)
        opening = b == 0 and c == 0
        if opening:
            y = jnp.dot(x, wv[b, :, :hid], preferred_element_type=jnp.float32)
            to[b, c] = y.astype(to.dtype)
            peers = sum(inside(place).astype(jnp.int32) for place in greeted)
            pl.semaphore_wait(barrier, peers)
            send_outer(b, c)
            fill_ends()
        once(w_load, b, 1)
        once(w_load, b, 2)
        if opening:
            y = jnp.dot(x, wv[b, :, hid:], preferred_element_type=jnp.float32)
        else:
            y = jnp.dot(x, wv[b], preferred_element_type=jnp.float32)
            to[b, c] = y[:, :hid].astype(to.dtype)
            send_outer(b, c)
            y = y[:, hid:]
        cen[c] = y[:, :hid]
        if relay(b):
            own[c] = y[:, hid:]
            return
        ti[b, c] = y[:, hid:].astype(ti.dtype)
        if c + steps[b] >= chunks:
            send(inner_copy(b, c, 2 * chunks - 1 - c - steps[b], inner))

    def pass_on(b, c):
        _, partner, target, source = places(b)

        @pl.when(inside(source))
        def _():
            outer_copy(b, c, c, target).wait_recv()
        ti[b, c] = (own[c] + ro[b, c].astype(jnp.float32)).astype(ti.dtype)
        send(inner_copy(b, c, c, partner))

    def mix(b, c):
        v = cen[c]
        step = steps[b]
        if relay(b):
            inner_copy(b, c, c, places(b)[1]).wait_recv()
            v = v + ri[b, c].astype(jnp.float32)
        else:
            if c + step < chunks:
                v = v + to[b, c + step].astype(jnp.float32)
            else:
                inner_copy(b, 2 * chunks - 1 - c - step, c, inner).wait_recv()
                v = v + ri[b, c].astype(jnp.float32)
            if c >= step:
                v = v + ti[b, c - step].astype(jnp.float32)
            else:
                @pl.when(inside(outer))
                def _():
                    outer_copy(b, step - 1 - c, c, outer).wait_recv()
                v = v + ro[b, c].astype(jnp.float32)
        once(p_load, b)
        hidden = jax.nn.gelu(v, approximate=True).astype(jnp.bfloat16)
        branch = jnp.dot(hidden, pv[b], preferred_element_type=jnp.float32)
        out[b, span(c), :] = (x_of(b, c).astype(jnp.float32) + branch).astype(out.dtype)

    for kind, b, c in plan(steps, chunks):
        {"taps": taps, "mix": mix, "pass": pass_on}[kind](b, c)

    for copy, place in sent:
        if place is None:
            copy.wait_send()
        else:
            @pl.when(inside(place))
            def _():
                copy.wait_send()


def plan(steps, chunks):
    blocks = len(steps)
    when = {("taps", 0, c): 0.0 for c in range(chunks)}
    done, order, clock = {}, [], 0.0
    wire = {"off": 0.0, "on": 0.0}
    jobs = [("taps", b, c) for b in range(blocks) for c in range(chunks)]
    jobs += [("mix", b, c) for b in range(blocks) for c in range(chunks)]
    jobs += [("pass", b, c) for b in range(blocks) for c in range(chunks) if steps[b] > chunks]
    arrive = {}

    def needs(job):
        kind, b, c = job
        step = steps[b]
        if kind == "taps":
            return [done.get(("mix", b - 1, c))] if b else [0.0]
        if kind == "pass":
            return [done.get(("taps", b, c)), arrive.get(("off", b, c))]
        if step > chunks:
            return [done.get(("taps", b, c)), arrive.get(("on", b, c))]
        got = [done.get(("taps", b, c))]
        got.append(done.get(("taps", b, c + step)) if c + step < chunks else arrive.get(("on", b, c)))
        got.append(done.get(("taps", b, c - step)) if c >= step else arrive.get(("off", b, c)))
        return got

    while jobs:
        best = None
        for job in jobs:
            got = needs(job)
            if None in got:
                continue
            start = max([clock] + got)
            kind, b, c = job
            key = (start, {"pass": 0, "taps": 1, "mix": 2}[kind] if b else 3, c if b == 0 else 0)
            if kind == "mix":
                outward = b + 1 < blocks and c < steps[b + 1]
                key = (start, 2 if outward else 4, c)
            if best is None or key < best[0]:
                best = (key, job)
        (start, *_), job = best
        kind, b, c = job
        step = steps[b]
        jobs.remove(job)
        order.append(job)
        clock = start + {"taps": 0.7, "mix": 0.4, "pass": 0.1}[kind]
        done[job] = clock

        def fly(way, d, cost):
            wire[way] = max(wire[way], clock) + cost
            arrive[(way, b, d)] = wire[way] + 1.5
        if kind == "pass":
            wire["off"] = max(wire["off"], clock) + 4.0
            arrive[("on", b, c)] = wire["off"] + 1.5
        elif kind == "taps" and step > chunks:
            arrive[("off", b, c)] = clock + 6.0
        elif kind == "taps":
            if c < step:
                fly("off", step - 1 - c, 4.0)
            if c + step >= chunks:
                fly("on", 2 * chunks - 1 - c - step, 0.5)
    return order


def shards(n, signal, dilated_tap_weight, point_weight):
    length, wide = signal.shape
    blocks, taps, _, hid = dilated_tap_weight.shape
    rows = min(FIRST_DILATION, length)
    chunks = length // rows
    steps = [FIRST_DILATION * 2**b // rows for b in range(blocks)]
    assert n % 2 == 0
    for step in steps:
        hop = step // chunks
        assert step <= chunks or (step % chunks == 0 and n % (2 * hop) == 0)
    bf16, f32 = jnp.bfloat16, jnp.float32
    terms = pltpu.VMEM((blocks, chunks, rows, hid), bf16)
    dma = pltpu.SemaphoreType.DMA
    return pl.pallas_call(
        functools.partial(kernel, n, steps),
        out_shape=pltpu.VMEM((blocks, length, wide), bf16),
        in_specs=[pl.BlockSpec(memory_space=pl.ANY)] * 3,
        out_specs=pl.BlockSpec(memory_space=pltpu.VMEM),
        scratch_shapes=[
            pltpu.VMEM((chunks, rows, wide), bf16),
            pltpu.VMEM((blocks, wide, taps * hid), bf16),
            pltpu.VMEM((blocks, hid, wide), bf16),
            pltpu.VMEM((chunks, rows, hid), f32),
            pltpu.VMEM((chunks, rows, hid), f32),
            terms, terms, terms, terms,
            dma((blocks, chunks)), dma((blocks, chunks)),
            dma((blocks, chunks)), dma((blocks, chunks)),
            dma((chunks,)), dma((blocks, taps)), dma((blocks,)),
        ],
        compiler_params=pltpu.CompilerParams(
            collective_id=0, has_side_effects=True, vmem_limit_bytes=48 * 2**20),
    )(signal, dilated_tap_weight, point_weight)


def solution(mesh):
    in_specs = (P(("grp", "seq"), None), P(), P())
    out_specs = P(None, ("grp", "seq"), None)
    return jax.shard_map(functools.partial(shards, mesh.shape["seq"]), mesh=mesh,
                         in_specs=in_specs, out_specs=out_specs, check_vma=False)
```

time: 61.4 us -> 55.3 us (0.901)
  local copies, waits for them, and re-layouts: 5.89 us -> 2.71 us
  Pallas kernels: 55.3 us -> 52.2 us
    unnamed x1, local copies, waits for them, and re-layouts: 5.89 us -> 2.71 us
    pallas_call x1, Pallas kernels: 55.3 us -> 52.2 us  [shards(): pl.pallas_call(functools.partial(kernel, n, steps), out_shape=pltpu.VMEM(...]
where the time goes in v2:
time: 55.3 us; the launch traced here: 54.9 us
  Pallas kernels  52.2 us (94%)
  local copies, waits for them, and re-layouts  2.71 us (5%)
    pallas_call x1, Pallas kernels, shards(): pl.pallas_call(functools.partial(kernel, n, steps), out_shape=pltpu.VMEM(...  52.2 us
    unnamed x1, local copies, waits for them, and re-layouts  2.71 us

profile of v2, /device:TPU:15, one launch (start us, length us, event | category | flops | bytes accessed | tf_op | source)
XLA Modules:
  0.0 54.9 jit_solution(17825607983606927776)
XLA Ops:
  0.0 52.2 %shard_map.37 = bf16[4,1024,768]{2,1,0:T(8,128)(2,1)S(1)} custom-call(bf16[1024,768]{1,0:T(8,128)(2,1)} %x_hbm.1, bf16[4,3,768,384]{3,2,1,0:T(8,128)(2,1)} %w_hbm.1, bf16[4,384,768]{2,1,0:T(8,128)(2,1)} %p_hbm.1), custom_call_target="tpu_custom_call" | custom-call | tf_op jit(solution)/shard_map/pallas_call | solution.py:282
  52.2 2.7 %copy.5 = bf16[4,1024,768]{2,1,0:T(8,128)(2,1)} copy(bf16[4,1024,768]{2,1,0:T(8,128)(2,1)S(1)} %shard_map.37) | data formatting | bytes 12582912

commit v3 on v2

--- a/solution.py
+++ b/solution.py
@@ -20,8 +20,8 @@
     return order
 
 
-def kernel(n, steps, x_hbm, w_hbm, p_hbm, out, xs, wv, pv, cen, own, to, ti, ro, ri,
-           send_o, send_i, recv_o, recv_i, sem_x, sem_w, sem_p):
+def kernel(n, steps, x_hbm, w_hbm, p_hbm, out, xs, wv, pv, cen, own, to, ti, ro, ri, held,
+           send_o, send_i, recv_o, recv_i, sem_x, sem_w, sem_p, send_h, recv_h):
     blocks = len(steps)
     chunks, rows = xs.shape[0], xs.shape[1]
     hid = p_hbm.shape[1]
@@ -49,6 +49,23 @@
         if relay(b):
             _, partner, target, source = places(b)
             greeted += [partner, target, source]
+    order = plan(steps, chunks)
+
+    side = lax.rem(lax.div(me, 2), 2)
+    beside = me + 2 - 4 * side
+    beyond = me - 3 + 6 * core
+    quads = n // 4
+    along = lax.div(me, 4)
+    along = along + core * (quads - 1 - 2 * along)
+    share = lax.div(along * chunks, quads)
+    if any(detour(steps, chunks, b) for b in range(blocks)):
+        greeted.append(beyond)
+
+    def detoured(b, c):
+        turn = [k for kind, at, k in order if kind == "taps" and at == b].index(c)
+        rank = (chunks - 2, *range(chunks - 2), chunks - 1)[turn]
+        return rank < share
+
     barrier = pltpu.get_barrier_semaphore()
     for place in greeted:
         @pl.when(inside(place))
@@ -74,13 +91,17 @@
     x_load(0).start()
     for t in range(3):
         w_load(0, t).start()
-    for c in range(1, chunks):
-        x_load(c).start()
-    p_load(0).start()
-    for b in range(1, blocks):
-        for t in range(3):
-            w_load(b, t).start()
-        p_load(b).start()
+
+    def load_block():
+        for c in range(1, chunks):
+            x_load(c).start()
+        p_load(0).start()
+
+    def load_rest():
+        for b in range(1, blocks):
+            for t in range(3):
+                w_load(b, t).start()
+            p_load(b).start()
 
     def fill_ends():
         for b in range(blocks):
@@ -100,6 +121,22 @@
         return pltpu.make_async_remote_copy(
             src_ref=ti.at[b, s], dst_ref=ri.at[b, d], send_sem=send_i.at[b, s],
             recv_sem=recv_i.at[b, d], device_id={"seq": place}, device_id_type=MESH)
+
+    def aside_copy(b, c):
+        return pltpu.make_async_remote_copy(
+            src_ref=to.at[b, c], dst_ref=held.at[c], send_sem=send_o.at[b, c],
+            recv_sem=recv_h.at[c], device_id={"seq": beside}, device_id_type=MESH)
+
+    def onward_copy(b, c):
+        return pltpu.make_async_remote_copy(
+            src_ref=held.at[c], dst_ref=ro.at[b, steps[b] - 1 - c], send_sem=send_h.at[c],
+            recv_sem=recv_o.at[b, steps[b] - 1 - c], device_id={"seq": beyond}, device_id_type=MESH)
+
+    def hand_on(b, c):
+        @pl.when(jnp.logical_and(side != core, detoured(b, c)))
+        def _():
+            aside_copy(b, c).wait_recv()
+            onward_copy(b, c).start()
 
     sent = []
 
@@ -119,6 +156,18 @@
         if relay(b):
             target = places(b)[2]
             send(outer_copy(b, c, c, target), target)
+        elif detour(steps, chunks, b):
+            around = jnp.logical_and(side == core, detoured(b, c))
+            straight = outer_copy(b, c, steps[b] - 1 - c, outer)
+
+            @pl.when(around)
+            def _():
+                aside_copy(b, c).start()
+
+            @pl.when(jnp.logical_and(inside(outer), jnp.logical_not(around)))
+            def _():
+                straight.start()
+            sent.append((straight, outer))
         elif c < steps[b]:
             send(outer_copy(b, c, steps[b] - 1 - c, outer), outer)
 
@@ -136,12 +185,14 @@
         once(w_load, b, 0)
         opening = b == 0 and c == 0
         if opening:
+            load_block()
             y = jnp.dot(x, wv[b, :, :hid], preferred_element_type=jnp.float32)
             to[b, c] = y.astype(to.dtype)
             peers = sum(inside(place).astype(jnp.int32) for place in greeted)
             pl.semaphore_wait(barrier, peers)
             send_outer(b, c)
             fill_ends()
+            load_rest()
         once(w_load, b, 1)
         once(w_load, b, 2)
         if opening:
@@ -192,8 +243,8 @@
         branch = jnp.dot(hidden, pv[b], preferred_element_type=jnp.float32)
         out[b, span(c), :] = (x_of(b, c).astype(jnp.float32) + branch).astype(out.dtype)
 
-    for kind, b, c in plan(steps, chunks):
-        {"taps": taps, "mix": mix, "pass": pass_on}[kind](b, c)
+    for kind, b, c in order:
+        {"taps": taps, "mix": mix, "pass": pass_on, "hand": hand_on}[kind](b, c)
 
     for copy, place in sent:
         if place is None:
@@ -202,6 +253,15 @@
             @pl.when(inside(place))
             def _():
                 copy.wait_send()
+    for kind, b, c in order:
+        if kind == "hand":
+            @pl.when(jnp.logical_and(side != core, detoured(b, c)))
+            def _():
+                onward_copy(b, c).wait_send()
+
+
+def detour(steps, chunks, b):
+    return chunks > 1 and steps[b] == chunks and 2 * chunks in steps
 
 
 def plan(steps, chunks):
@@ -212,11 +272,14 @@
     jobs = [("taps", b, c) for b in range(blocks) for c in range(chunks)]
     jobs += [("mix", b, c) for b in range(blocks) for c in range(chunks)]
     jobs += [("pass", b, c) for b in range(blocks) for c in range(chunks) if steps[b] > chunks]
+    jobs += [("hand", b, c) for b in range(blocks) for c in range(chunks) if detour(steps, chunks, b)]
     arrive = {}
 
     def needs(job):
         kind, b, c = job
         step = steps[b]
+        if kind == "hand":
+            return [arrive.get(("hand", b, c))]
         if kind == "taps":
             return [done.get(("mix", b - 1, c))] if b else [0.0]
         if kind == "pass":
@@ -236,7 +299,7 @@
                 continue
             start = max([clock] + got)
             kind, b, c = job
-            key = (start, {"pass": 0, "taps": 1, "mix": 2}[kind] if b else 3, c if b == 0 else 0)
+            key = (start, {"hand": 0, "pass": 0, "taps": 1, "mix": 2}[kind] if b else 3, c if b == 0 else 0)
             if kind == "mix":
                 outward = b + 1 < blocks and c < steps[b + 1]
                 key = (start, 2 if outward else 4, c)
@@ -247,7 +310,7 @@
         step = steps[b]
         jobs.remove(job)
         order.append(job)
-        clock = start + {"taps": 0.7, "mix": 0.4, "pass": 0.1}[kind]
+        clock = start + {"taps": 0.7, "mix": 0.4, "pass": 0.1, "hand": 0.0}[kind]
         done[job] = clock
 
         def fly(way, d, cost):
@@ -261,6 +324,8 @@
         elif kind == "taps":
             if c < step:
                 fly("off", step - 1 - c, 4.0)
+                if detour(steps, chunks, b):
+                    arrive[("hand", b, c)] = max(clock, arrive[("off", b, step - 1 - c)] - 4.0)
             if c + step >= chunks:
                 fly("on", 2 * chunks - 1 - c - step, 0.5)
     return order
@@ -291,9 +356,11 @@
             pltpu.VMEM((chunks, rows, hid), f32),
             pltpu.VMEM((chunks, rows, hid), f32),
             terms, terms, terms, terms,
+            pltpu.VMEM((chunks, rows, hid), bf16),
             dma((blocks, chunks)), dma((blocks, chunks)),
             dma((blocks, chunks)), dma((blocks, chunks)),
             dma((chunks,)), dma((blocks, taps)), dma((blocks,)),
+            dma((chunks,)), dma((chunks,)),
         ],
         compiler_params=pltpu.CompilerParams(
             collective_id=0, has_side_effects=True, vmem_limit_bytes=48 * 2**20),

time: 55.3 us -> 53 us (0.958)
  Pallas kernels: 52.2 us -> 49.8 us
    pallas_call x1, Pallas kernels: 52.2 us -> 49.8 us  [shards(): pl.pallas_call(functools.partial(kernel, n, steps), out_shape=pltpu.VMEM(...]
where the time goes in v3:
time: 53 us; the launch traced here: 52.5 us
  Pallas kernels  49.8 us (94%)
  local copies, waits for them, and re-layouts  2.71 us (5%)
    pallas_call x1, Pallas kernels, shards(): pl.pallas_call(functools.partial(kernel, n, steps), out_shape=pltpu.VMEM(...  49.8 us
    unnamed x1, local copies, waits for them, and re-layouts  2.71 us

profile of v3, /device:TPU:15, one launch (start us, length us, event | category | flops | bytes accessed | tf_op | source)
XLA Modules:
  0.0 52.5 jit_solution(5845688773678770785)
XLA Ops:
  0.0 49.8 %shard_map.37 = bf16[4,1024,768]{2,1,0:T(8,128)(2,1)S(1)} custom-call(bf16[1024,768]{1,0:T(8,128)(2,1)} %x_hbm.1, bf16[4,3,768,384]{3,2,1,0:T(8,128)(2,1)} %w_hbm.1, bf16[4,384,768]{2,1,0:T(8,128)(2,1)} %p_hbm.1), custom_call_target="tpu_custom_call" | custom-call | tf_op jit(solution)/shard_map/pallas_call | solution.py:347
  49.8 2.7 %copy.5 = bf16[4,1024,768]{2,1,0:T(8,128)(2,1)} copy(bf16[4,1024,768]{2,1,0:T(8,128)(2,1)S(1)} %shard_map.37) | data formatting | bytes 12582912
